TPU v7x, 32 devices: a whole 2x2x4 slice. The times are simulated.
32 devices in a mesh: ray: 4 (over z), cell: 8 (over y, x, core).
Axes of the slice: x: 2, y: 2, z: 4, core: 2. Of those that a mesh axis runs over, the one named last changes fastest.
Arguments:
- right_side: float32 [8, 8192], P(None, 'ray'), may hold values from -6 to 6
- tiles: bfloat16 [32, 32, 256, 256], P('ray', 'cell'), may hold values from -0.375 to 0.375
- pattern: int32 [32, 32], P('ray', 'cell'), may hold values from 0 to 31, as said below
- counts: int32 [32, 8], P('ray', 'cell'), may hold values from 1 to 4, as said below
Outputs:
- solution: float32 [8, 65536], P(None, 'cell')
- misfit: float32 [8], replicated
Inputs may be any that keep to these rules, and one draw needn't show every extreme that they name: `pattern`: each entry indexes a block within the slot's group of 32 cell blocks; a bundle may name a block more than once. Ragged counts; some bundle has all 4 slots live in some group, and some has one.
All inputs are finite; a program needn't handle non-finite values.
Results may differ from a plain program's by a relative error of at most 0.0014.
Values may be sent and summed in bfloat16 or wider, within the bound.
A program may use at most 64 MiB of HBM per device.

v0:
```python
import jax
import jax.numpy as jnp
from jax import lax
from jax.sharding import PartitionSpec as P

BLK_DEV = 32
ITERS = 4


def norm_rows(local_sq):
    total = lax.psum(local_sq, "ray")
    return jnp.sqrt(total + 1e-06)


def norm_cols(local_sq):
    total = lax.psum(local_sq, "cell")
    return jnp.sqrt(total + 1e-06)


def local(right_side, tiles, pattern, counts):
    nrhs = right_side.shape[0]
    bundles = tiles.shape[0]
    slots = tiles.shape[1]
    ray_rows = tiles.shape[2]
    block_cells = tiles.shape[3]
    blocks = BLK_DEV
    live = lax.broadcasted_iota(jnp.int32, pattern.shape, 1) < counts
    live_bf = live.astype(jnp.bfloat16)
    selector = (
        (pattern[:, :, None] == lax.broadcasted_iota(jnp.int32, (bundles, slots, blocks), 2))
        & live[:, :, None]
    ).astype(jnp.float32)

    def adjoint(vector_bf):
        rows = vector_bf.reshape(nrhs, bundles, ray_rows)
        per = jnp.einsum("bsrc,nbr->bsnc", tiles, rows, preferred_element_type=jnp.float32)
        total = jnp.einsum("bsk,bsnc->nkc", selector, per, precision=lax.Precision.HIGHEST)
        return total.reshape(nrhs, blocks * block_cells)

    u_state = right_side
    beta = norm_rows(jnp.sum(u_state * u_state, axis=1))
    u_state = u_state / beta[:, None]

    def rows_bf(state):
        return state.astype(jnp.bfloat16)

    def cols_reduce(adj_terms):
        return lax.psum(adj_terms, "ray")

    v_state = cols_reduce(adjoint(rows_bf(u_state)))
    alpha = norm_cols(jnp.sum(v_state * v_state, axis=1))
    v_state = v_state / alpha[:, None]
    w_state = v_state
    x_state = jnp.zeros_like(v_state)
    phibar = beta
    rhobar = alpha
    for step in range(ITERS):
        vblocks = v_state.astype(jnp.bfloat16).reshape(nrhs, blocks, block_cells)
        picked = vblocks[:, pattern] * live_bf[None, :, :, None]
        partial_value = jnp.einsum(
            "bsrc,nbsc->nbr", tiles, picked, preferred_element_type=jnp.float32
        )
        partial_value = partial_value.reshape(nrhs, bundles * ray_rows)
        summed = lax.psum(partial_value, "cell")
        u_state = summed - alpha[:, None] * u_state
        beta = norm_rows(jnp.sum(u_state * u_state, axis=1))
        u_state = u_state / beta[:, None]
        v_state = cols_reduce(adjoint(rows_bf(u_state))) - beta[:, None] * v_state
        alpha = norm_cols(jnp.sum(v_state * v_state, axis=1))
        v_state = v_state / alpha[:, None]
        rho = jnp.sqrt(rhobar * rhobar + beta * beta)
        cosine = rhobar / rho
        sine = beta / rho
        theta = sine * alpha
        rhobar = -cosine * alpha
        phi = cosine * phibar
        phibar = sine * phibar
        x_state = x_state + (phi / rho)[:, None] * w_state
        w_state = v_state - (theta / rho)[:, None] * w_state
    return (x_state, phibar)


def solution(mesh):
    in_specs = (P(None, "ray"), P("ray", "cell", None, None), P("ray", "cell"), P("ray", "cell"))
    out_specs = (P(None, "cell"), P())
    return jax.shard_map(local, mesh=mesh, in_specs=in_specs, out_specs=out_specs, check_vma=False)
```

profile of v0, /device:TPU:0, one launch (start us, length us, event | category | flops | bytes accessed | tf_op | source)
XLA Modules:
  0.0 515.1 jit_solution(9101913132747717034)
XLA Ops:
  7.2 1.0 multiply_reduce_fusion.8
  8.2 13.5 %psum.119 = f32[8]{0:T(128)S(1)} all-reduce(f32[8]{0:T(128)S(1)} %multiply_reduce_fusion.8), channel_id=1, replica_groups=mesh['ray'=4,'cell'=8] {'ray'}, use_global_device_ids=true, to_apply=%region_1.0 | all-reduce | flops 8 | bytes 64 | tf_op jit(solution)/shard_map/psum | solution.py:11
  21.7 0.7 fusion.33
  22.5 0.9 fusion.27
  23.4 2.8 fusion.51
  26.7 0.9 copy.26
  27.9 33.7 %all-reduce.9.cloned.1.call-done = f32[8,8192]{1,0:T(8,128)} async-done(((f32[8,8192]{1,0:T(8,128)}), f32[8,8192]{1,0:T(8,128)}) %all-reduce.9.cloned.1.call-update) | async-done | bytes 262160 | tf_op jit(solution)/shard_map/psum | solution.py:48
  61.6 1.1 multiply_reduce_fusion.3
  62.7 11.8 %psum.121 = f32[8]{0:T(128)S(1)} all-reduce(f32[8]{0:T(128)S(1)} %multiply_reduce_fusion.3), channel_id=1, replica_groups=mesh['ray'=4,'cell'=8] {'cell'}, use_global_device_ids=true, to_apply=%region_4.0 | all-reduce | flops 8 | bytes 64 | tf_op jit(solution)/shard_map/psum | solution.py:16
  74.5 1.0 fusion.42
  75.6 0.6 gather_fusion
  76.2 4.1 fusion.14
  80.3 52.3 %all-reduce.11.cloned.1.call-done = f32[8,2048]{1,0:T(8,128)} async-done(((f32[8,2048]{1,0:T(8,128)}), f32[8,2048]{1,0:T(8,128)}) %all-reduce.11.cloned.1.call-update) | async-done | bytes 65552 | tf_op jit(solution)/shard_map/psum | solution.py:64
  132.6 1.0 multiply_reduce_fusion.7
  133.6 11.7 %psum.123 = f32[8]{0:T(128)S(1)} all-reduce(f32[8]{0:T(128)S(1)} %get-tuple-element.21), channel_id=1, replica_groups=mesh['ray'=4,'cell'=8] {'ray'}, use_global_device_ids=true, to_apply=%region_7.0 | all-reduce | flops 8 | bytes 64 | tf_op jit(solution)/shard_map/psum | solution.py:11
  145.4 2.8 fusion.52
  148.7 0.9 copy.27
  149.7 32.3 %all-reduce.13.cloned.1.call-done = f32[8,8192]{1,0:T(8,128)} async-done(((f32[8,8192]{1,0:T(8,128)}), f32[8,8192]{1,0:T(8,128)}) %all-reduce.13.cloned.1.call-update) | async-done | bytes 262160 | tf_op jit(solution)/shard_map/psum | solution.py:48
  182.0 1.2 multiply_reduce_fusion.2
  183.2 11.8 %psum.125 = f32[8]{0:T(128)S(1)} all-reduce(f32[8]{0:T(128)S(1)} %multiply_reduce_fusion.2), channel_id=1, replica_groups=mesh['ray'=4,'cell'=8] {'cell'}, use_global_device_ids=true, to_apply=%region_10.0 | all-reduce | flops 8 | bytes 64 | tf_op jit(solution)/shard_map/psum | solution.py:16
  195.0 1.1 fusion.50
  196.1 0.6 gather_fusion.1
  196.7 4.0 fusion.12
  200.8 52.3 %all-reduce.15.cloned.1.call-done = f32[8,2048]{1,0:T(8,128)} async-done(((f32[8,2048]{1,0:T(8,128)}), f32[8,2048]{1,0:T(8,128)}) %all-reduce.15.cloned.1.call-update) | async-done | bytes 65552 | tf_op jit(solution)/shard_map/psum | solution.py:64
  253.0 1.0 multiply_reduce_fusion.6
  254.1 11.7 %psum.127 = f32[8]{0:T(128)S(1)} all-reduce(f32[8]{0:T(128)S(1)} %get-tuple-element.17), channel_id=1, replica_groups=mesh['ray'=4,'cell'=8] {'ray'}, use_global_device_ids=true, to_apply=%region_13.0 | all-reduce | flops 8 | bytes 64 | tf_op jit(solution)/shard_map/psum | solution.py:11
  265.9 2.8 fusion.53
  269.2 0.9 copy.28
  270.1 32.3 %all-reduce.17.cloned.1.call-done = f32[8,8192]{1,0:T(8,128)} async-done(((f32[8,8192]{1,0:T(8,128)}), f32[8,8192]{1,0:T(8,128)}) %all-reduce.17.cloned.1.call-update) | async-done | bytes 262160 | tf_op jit(solution)/shard_map/psum | solution.py:48
  302.4 1.2 multiply_reduce_fusion.1
  303.6 11.8 %psum.129 = f32[8]{0:T(128)S(1)} all-reduce(f32[8]{0:T(128)S(1)} %multiply_reduce_fusion.1), channel_id=1, replica_groups=mesh['ray'=4,'cell'=8] {'cell'}, use_global_device_ids=true, to_apply=%region_16.0 | all-reduce | flops 8 | bytes 64 | tf_op jit(solution)/shard_map/psum | solution.py:16
  315.4 1.1 fusion.49
  317.1 4.0 fusion.10
  321.2 52.3 %all-reduce.19.cloned.1.call-done = f32[8,2048]{1,0:T(8,128)} async-done(((f32[8,2048]{1,0:T(8,128)}), f32[8,2048]{1,0:T(8,128)}) %all-reduce.19.cloned.1.call-update) | async-done | bytes 65552 | tf_op jit(solution)/shard_map/psum | solution.py:64
  373.5 1.0 multiply_reduce_fusion.5
  374.5 11.7 %psum.131 = f32[8]{0:T(128)S(1)} all-reduce(f32[8]{0:T(128)S(1)} %get-tuple-element.13), channel_id=1, replica_groups=mesh['ray'=4,'cell'=8] {'ray'}, use_global_device_ids=true, to_apply=%region_19.0 | all-reduce | flops 8 | bytes 64 | tf_op jit(solution)/shard_map/psum | solution.py:11
  386.3 2.8 fusion.54
  389.6 0.9 copy.29
  390.5 32.3 %all-reduce.21.cloned.1.call-done = f32[8,8192]{1,0:T(8,128)} async-done(((f32[8,8192]{1,0:T(8,128)}), f32[8,8192]{1,0:T(8,128)}) %all-reduce.21.cloned.1.call-update) | async-done | bytes 262160 | tf_op jit(solution)/shard_map/psum | solution.py:48
  422.8 1.3 multiply_reduce_fusion
  424.1 11.8 %psum.133 = f32[8]{0:T(128)S(1)} all-reduce(f32[8]{0:T(128)S(1)} %multiply_reduce_fusion), channel_id=1, replica_groups=mesh['ray'=4,'cell'=8] {'cell'}, use_global_device_ids=true, to_apply=%region_22.0 | all-reduce | flops 8 | bytes 64 | tf_op jit(solution)/shard_map/psum | solution.py:16
  435.9 1.1 fusion.24
  437.6 4.0 fusion.8
  441.6 52.3 %all-reduce.23.cloned.1.call-done = f32[8,2048]{1,0:T(8,128)} async-done(((f32[8,2048]{1,0:T(8,128)}), f32[8,2048]{1,0:T(8,128)}) %all-reduce.23.cloned.1.call-update) | async-done | bytes 65552 | tf_op jit(solution)/shard_map/psum | solution.py:64
  493.9 1.0 multiply_reduce_fusion.4
  495.0 11.7 %psum.135 = f32[8]{0:T(128)S(1)} all-reduce(f32[8]{0:T(128)S(1)} %multiply_reduce_fusion.4), channel_id=1, replica_groups=mesh['ray'=4,'cell'=8] {'ray'}, use_global_device_ids=true, to_apply=%region_25.0 | all-reduce | flops 8 | bytes 64 | tf_op jit(solution)/shard_map/psum | solution.py:11
  506.7 0.6 divide_multiply_fusion
  507.3 0.9 multiply_add_fusion
  (47 shorter events, 4.1 us)
Async XLA Ops:
  7.2 19.1 %copy-start.3 = (s32[8,4]{0,1:T(4,128)S(1)}, s32[8,4]{0,1:T(4,128)}, u32[]{:S(2)}) copy-start(s32[8,4]{0,1:T(4,128)} %param.6) | copy-start | bytes 388
  7.2 54.4 %all-reduce.9.cloned.1.call-start = ((), (), s32[]{:S(2)}) async-start(), calls=%async_computation | async-start | bytes 524288 | tf_op jit(solution)/shard_map/psum | solution.py:48
  26.3 106.3 %copy-start.2 = (f32[8,2048]{1,0:T(8,128)S(1)}, f32[8,2048]{1,0:T(8,128)}, u32[]{:S(2)}) copy-start(f32[8,2048]{1,0:T(8,128)} %param.4) | copy-start | bytes 196612
  27.6 105.0 %all-reduce.11.cloned.1.call-start = ((), (), s32[]{:S(2)}) async-start(), calls=%async_computation.1 | async-start | bytes 131072 | tf_op jit(solution)/shard_map/psum | solution.py:64
  76.2 105.8 %copy-start = (f32[8,8192]{1,0:T(8,128)S(1)}, f32[8,8192]{1,0:T(8,128)}, u32[]{:S(2)}) copy-start(f32[8,8192]{1,0:T(8,128)} %all-reduce.9.cloned.1.call-done) | copy-start | bytes 786436
  80.3 101.7 %all-reduce.13.cloned.1.call-start = ((), (), s32[]{:S(2)}) async-start(), calls=%async_computation.2 | async-start | bytes 524288 | tf_op jit(solution)/shard_map/psum | solution.py:48
  149.6 103.4 %all-reduce.15.cloned.1.call-start = ((), (), s32[]{:S(2)}) async-start(), calls=%async_computation.3 | async-start | bytes 131072 | tf_op jit(solution)/shard_map/psum | solution.py:64
  200.7 101.7 %all-reduce.17.cloned.1.call-start = ((), (), s32[]{:S(2)}) async-start(), calls=%async_computation.4 | async-start | bytes 524288 | tf_op jit(solution)/shard_map/psum | solution.py:48
  270.1 103.4 %all-reduce.19.cloned.1.call-start = ((), (), s32[]{:S(2)}) async-start(), calls=%async_computation.5 | async-start | bytes 131072 | tf_op jit(solution)/shard_map/psum | solution.py:64
  321.1 101.7 %all-reduce.21.cloned.1.call-start = ((), (), s32[]{:S(2)}) async-start(), calls=%async_computation.6 | async-start | bytes 524288 | tf_op jit(solution)/shard_map/psum | solution.py:48
  390.5 103.5 %all-reduce.23.cloned.1.call-start = ((), (), s32[]{:S(2)}) async-start(), calls=%async_computation.7 | async-start | bytes 131072 | tf_op jit(solution)/shard_map/psum | solution.py:64
  422.8 84.5 %copy-start.1 = (f32[8,8192]{1,0:T(8,128)S(1)}, f32[8,8192]{1,0:T(8,128)}, u32[]{:S(2)}) copy-start(f32[8,8192]{1,0:T(8,128)} %all-reduce.21.cloned.1.call-done) | copy-start | bytes 786436
Sparse Core Ops, SparseCore 0:
  27.7 33.7 all-reduce.8
  80.4 52.1 all-reduce.10
  149.7 32.1 all-reduce.12
  200.8 52.1 all-reduce.14
  270.2 32.1 all-reduce.16
  321.3 52.1 all-reduce.18
  390.6 32.1 all-reduce.20
  441.7 52.1 all-reduce.22
where the time goes:
time: 516 us; the launch traced here: 515 us
  waiting for transfers between devices  340 us (66%)
  blocking collectives  108 us (21%)
  matrix products  29.3 us (6%)
  other arithmetic  17.7 us (3%)
  between operations  14.3 us (3%)
  local copies, waits for them, and re-layouts  5.99 us (1%)
    psum x4, waiting for transfers between devices, local(): summed = lax.psum(partial_value, 'cell')  209 us
    psum x4, waiting for transfers between devices, cols_reduce(): return lax.psum(adj_terms, 'ray')  131 us
    psum x5, blocking collectives, norm_rows(): total = lax.psum(local_sq, 'ray')  60.2 us
    psum x4, blocking collectives, norm_cols(): total = lax.psum(local_sq, 'cell')  47.3 us
    dot_general x4, matrix products, local(): jnp.einsum('bsrc,nbsc->nbr', tiles, picked, preferred_element_type=jnp.fl...  16.1 us
    dot_general x4, matrix products, adjoint(): jnp.einsum('bsrc,nbr->bsnc', tiles, rows, preferred_element_type=jnp.floa...  11.4 us
  transfers between devices with their start and end apart: 8, of which 8 were waited for; matrix products, arithmetic and copies ran while one was open for 0% of the time, Pallas kernels for 0%

commit v1 on v0

v1 whole, which is shorter than its diff:
```python
import functools

import jax
import jax.numpy as jnp
from jax import lax
from jax.experimental import pallas as pl
from jax.experimental.pallas import tpu as pltpu
from jax.sharding import PartitionSpec as P

BLK_DEV = 32
ITERS = 4
EPS = 1e-06
F32 = jnp.float32
BF16 = jnp.bfloat16


def split(value):
    hi = value.astype(BF16)
    lo = (value - hi.astype(F32)).astype(BF16)
    return hi, lo


def wide(stat, lanes):
    return jnp.broadcast_to(stat[:, 0:1], (stat.shape[0], lanes))


def row_sum(value):
    total = jnp.sum(value, axis=1, keepdims=True)
    return jnp.broadcast_to(total, (value.shape[0], 128))


def kernel(
    R, C,
    pattern, counts, rhs, tiles_hbm,
    out, mis,
    tiles, fpart, frecv, ucat, apart, arecv, vhi, vlo, vsh, usq, vsq, cum, w, x,
    idx, prv, lst,
    tile_sem, fs, fr, us, ur, as_, ar, ns, nr, hs, hr, ls, lr, qs, qr,
):
    B, S = pattern.shape
    N = rhs.shape[0]
    RB, CB = tiles.shape[2], tiles.shape[3]
    RC = rhs.shape[1] // C
    NCH = C // B
    NB = BLK_DEV
    K = NB // R
    slots = B * S
    me_r = lax.axis_index("ray")
    me_c = lax.axis_index("cell")

    loads = []
    for b in range(B):
        load = pltpu.make_async_copy(tiles_hbm.at[b], tiles.at[b], tile_sem.at[b])
        load.start()
        loads.append(load)

    barrier = pltpu.get_barrier_semaphore()
    for d in range(1, C):
        pl.semaphore_signal(barrier, inc=1, device_id={"cell": lax.rem(me_c + d, C)}, device_id_type=pl.DeviceIdType.MESH)
    for d in range(1, R):
        pl.semaphore_signal(barrier, inc=1, device_id={"ray": lax.rem(me_r + d, R)}, device_id_type=pl.DeviceIdType.MESH)

    def remote(src, dst, send, recv, axis, peer):
        return pltpu.make_async_remote_copy(
            src_ref=src, dst_ref=dst, send_sem=send, recv_sem=recv,
            device_id={axis: peer}, device_id_type=pl.DeviceIdType.MESH,
        )

    for b in range(B):
        for s in range(S):
            idx[b * S + s] = jnp.where(s < counts[b, 0], pattern[b, s], NB)

    def chain(i, carry):
        p = idx[i]
        found = jnp.int32(slots)
        for j in range(slots):
            found = jnp.where((idx[j] == p) & (j < i), j, found)
        prv[i] = found
        return carry

    lax.fori_loop(0, slots, chain, 0)

    def final(k, carry):
        found = jnp.int32(slots)
        for j in range(slots):
            found = jnp.where(idx[j] == k, j, found)
        lst[k] = found
        return carry

    lax.fori_loop(0, NB, final, 0)

    cum[slots] = jnp.zeros((N, CB), F32)
    vhi[NB] = jnp.zeros((N, CB), BF16)
    w[...] = jnp.zeros_like(w)
    x[...] = jnp.zeros_like(x)
    vsh[...] = jnp.zeros_like(vsh)
    for j in range(C):
        hi, lo = split(rhs[:, j * RC:(j + 1) * RC])
        ucat[j, 0:N] = hi
        ucat[j, N:2 * N] = lo

    pl.semaphore_wait(barrier, (C - 1) + (R - 1))

    def ray_copies(src, dst, send, recv, d, kind):
        peer = lax.rem(me_r + d, R)
        source = lax.rem(me_r + R - d, R)
        if kind == "scatter":
            s = src.at[pl.ds(peer * K, K)]
            t = dst.at[me_r]
        elif kind == "gather":
            s = src.at[pl.ds(me_r * K, K)]
            t = dst.at[pl.ds(me_r * K, K)]
        else:
            s = src.at[me_r]
            t = dst.at[me_r]
        return remote(s, t, send.at[d], recv.at[d], "ray", peer)

    order = sorted(range(1, R), key=lambda d: abs(d - R // 2))

    def norm_start():
        sq = jnp.zeros((N, RC), F32)
        for j in range(C):
            u = ucat[j, 0:N].astype(F32) + ucat[j, N:2 * N].astype(F32)
            sq = sq + u * u
        usq[me_r] = row_sum(sq)
        copies = [ray_copies(usq, usq, ns, nr, d, "slot") for d in order]
        for copy in copies:
            copy.start()
        return copies

    def norm_end(copies):
        for copy in copies:
            copy.wait()
        total = usq[0]
        for r in range(1, R):
            total = total + usq[r]
        return jnp.sqrt(total + EPS)

    def adjoint(wait):
        for b in range(B):
            if wait:
                loads[b].wait()
            if NCH == 1:
                rows = ucat[b]
            else:
                rows = jnp.concatenate([ucat[b * NCH + h] for h in range(NCH)], axis=1)
            for s in range(S):
                i = b * S + s
                per = lax.dot_general(rows, tiles[b, s], (((1,), (0,)), ((), ())), preferred_element_type=F32)
                cum[i] = per[0:N] + per[N:2 * N] + cum[prv[i]]
        for k in range(NB):
            apart[k] = cum[lst[k]]

    def scatter():
        copies = [ray_copies(apart, arecv, as_, ar, d, "scatter") for d in order]
        for copy in copies:
            copy.start()
        arecv[me_r] = apart[pl.ds(me_r * K, K)]
        for copy in copies:
            copy.wait()

    def gather_start(beta, alpha):
        inv = wide(1.0 / beta, CB)
        back = wide(beta / alpha, CB)
        sq = jnp.zeros((N, CB), F32)
        for k in range(K):
            total = arecv[0, k]
            for r in range(1, R):
                total = total + arecv[r, k]
            v = total * inv - back * vsh[k]
            vsh[k] = v
            sq = sq + v * v
            hi, lo = split(v)
            vhi[me_r * K + k] = hi
            vlo[me_r * K + k] = lo
        vsq[me_r] = row_sum(sq)
        first = [ray_copies(vhi, vhi, hs, hr, d, "gather") for d in order]
        first += [ray_copies(vsq, vsq, qs, qr, d, "slot") for d in order]
        second = [ray_copies(vlo, vlo, ls, lr, d, "gather") for d in order]
        for copy in first + second:
            copy.start()
        return first, second

    def low_copies():
        return [ray_copies(vlo, vlo, ls, lr, d, "gather") for d in order]

    def forward(beta, cosine, sine, rho):
        group = vsq[0]
        for r in range(1, R):
            group = group + vsq[r]
        mine = me_c // NCH
        for t in range(B):
            b = lax.rem(mine + 1 + t, B)
            acc = jnp.zeros((N, RB), F32)
            for s in range(S):
                acc = acc + lax.dot_general(
                    vhi[idx[b * S + s]], tiles[b, s], (((1,), (1,)), ((), ())), preferred_element_type=F32
                )
            for h in range(NCH):
                j = b * NCH + h
                fpart[j, :, 0:RC] = acc[:, h * RC:(h + 1) * RC]
                fpart[j, :, RC:RC + 128] = group
                d = lax.rem(j - me_c + C, C)

                @pl.when(j != me_c)
                def _():
                    remote(fpart.at[j], frecv.at[me_c], fs.at[d], fr.at[d], "cell", j).start()

        frecv[me_c] = fpart[me_c]
        for d in range(1, C):
            peer = lax.rem(me_c + d, C)
            remote(fpart.at[peer], frecv.at[me_c], fs.at[d], fr.at[d], "cell", peer).wait()
        total = frecv[0]
        for j in range(1, C):
            total = total + frecv[j]
        alpha = jnp.sqrt(total[:, RC:RC + 128] + EPS)
        old = ucat[me_c, 0:N].astype(F32) + ucat[me_c, N:2 * N].astype(F32)
        u = total[:, 0:RC] * wide(1.0 / alpha, RC) - wide(alpha / beta, RC) * old
        hi, lo = split(u)
        ucat[me_c, 0:N] = hi
        ucat[me_c, N:2 * N] = lo
        copies = []
        for d in range(1, C):
            peer = lax.rem(me_c + d, C)
            copies.append(remote(ucat.at[me_c], ucat.at[me_c], us.at[d], ur.at[d], "cell", peer))
        for copy in copies:
            copy.start()
        for copy in low_copies():
            copy.wait()
        theta = sine * alpha
        rhobar = -cosine * alpha
        inv = wide(1.0 / alpha, CB)
        ratio = wide(theta / rho, CB)
        for k in range(NB):
            w[k] = (vhi[k].astype(F32) + vlo[k].astype(F32)) * inv - ratio * w[k]
        for copy in copies:
            copy.wait()
        return alpha, rhobar

    def rotate(beta, rhobar, phibar):
        rho = jnp.sqrt(rhobar * rhobar + beta * beta)
        cosine = rhobar / rho
        sine = beta / rho
        phi = cosine * phibar
        return rho, cosine, sine, sine * phibar, phi / rho

    def step_x(step):
        scale = wide(step, CB)
        for k in range(NB):
            x[k] = x[k] + scale * w[k]

    norms = norm_start()
    adjoint(True)
    scatter()
    beta = norm_end(norms)
    one = jnp.ones((N, 128), F32)
    first, _ = gather_start(beta, one)
    for copy in first:
        copy.wait()

    def body(_, carry):
        beta, cosine, sine, rho, phibar = carry
        alpha, rhobar = forward(beta, cosine, sine, rho)
        norms = norm_start()
        adjoint(False)
        scatter()
        beta = norm_end(norms)
        first, _ = gather_start(beta, alpha)
        rho, cosine, sine, phibar, step = rotate(beta, rhobar, phibar)
        step_x(step)
        for copy in first:
            copy.wait()
        return beta, cosine, sine, rho, phibar

    carry = (beta, -one, jnp.zeros((N, 128), F32), one, beta)
    beta, cosine, sine, rho, phibar = lax.fori_loop(0, ITERS - 1, body, carry)
    alpha, rhobar = forward(beta, cosine, sine, rho)
    beta = norm_end(norm_start())
    rho, cosine, sine, phibar, step = rotate(beta, rhobar, phibar)
    scale = wide(step, CB)
    for k in range(NB):
        out[:, k * CB:(k + 1) * CB] = x[k] + scale * w[k]
    mis[...] = phibar


def local(R, C, right_side, tiles, pattern, counts):
    N, rows = right_side.shape
    B, S, RB, CB = tiles.shape
    NB = BLK_DEV
    RC = rows // C
    K = NB // R
    slots = B * S
    vmem = pl.BlockSpec(memory_space=pltpu.VMEM)
    smem = pl.BlockSpec(memory_space=pltpu.SMEM)
    dma = pltpu.SemaphoreType.DMA
    x, mis = pl.pallas_call(
        functools.partial(kernel, R, C),
        out_shape=(
            jax.ShapeDtypeStruct((N, NB * CB), F32),
            jax.ShapeDtypeStruct((N, 128), F32),
        ),
        in_specs=[smem, smem, vmem, pl.BlockSpec(memory_space=pl.ANY)],
        out_specs=(vmem, vmem),
        scratch_shapes=[
            pltpu.VMEM((B, S, RB, CB), BF16),
            pltpu.VMEM((C, N, RC + 128), F32),
            pltpu.VMEM((C, N, RC + 128), F32),
            pltpu.VMEM((C, 2 * N, RC), BF16),
            pltpu.VMEM((NB, N, CB), F32),
            pltpu.VMEM((R, K, N, CB), F32),
            pltpu.VMEM((NB + 1, N, CB), BF16),
            pltpu.VMEM((NB, N, CB), BF16),
            pltpu.VMEM((K, N, CB), F32),
            pltpu.VMEM((R, N, 128), F32),
            pltpu.VMEM((R, N, 128), F32),
            pltpu.VMEM((slots + 1, N, CB), F32),
            pltpu.VMEM((NB, N, CB), F32),
            pltpu.VMEM((NB, N, CB), F32),
            pltpu.SMEM((slots,), jnp.int32),
            pltpu.SMEM((slots,), jnp.int32),
            pltpu.SMEM((NB,), jnp.int32),
            dma((B,)),
            dma((C,)), dma((C,)), dma((C,)), dma((C,)),
            dma((R,)), dma((R,)), dma((R,)), dma((R,)),
            dma((R,)), dma((R,)), dma((R,)), dma((R,)),
            dma((R,)), dma((R,)),
        ],
        compiler_params=pltpu.CompilerParams(collective_id=0, has_side_effects=True),
    )(pattern, counts, right_side, tiles)
    return x, mis[:, 0]


def solution(mesh):
    R, C = mesh.shape["ray"], mesh.shape["cell"]
    in_specs = (P(None, "ray"), P("ray", "cell", None, None), P("ray", "cell"), P("ray", "cell"))
    out_specs = (P(None, "cell"), P())
    return jax.shard_map(
        functools.partial(local, R, C), mesh=mesh, in_specs=in_specs, out_specs=out_specs, check_vma=False
    )
```

time: 516 us -> 112 us (0.22)
  waiting for transfers between devices: 340 us -> 0 us
  blocking collectives: 108 us -> 0 us
  Pallas kernels: 0 us -> 105 us
  matrix products: 29.3 us -> 0 us
  other arithmetic: 17.7 us -> 0 us
  between operations: 14.3 us -> 0.64 us
    psum x8 -> x0, waiting for transfers between devices: 340 us -> none  [the longest x4 209 us: local(): summed = lax.psum(partial_value, 'cell')]
    psum x9 -> x0, blocking collectives: 108 us -> none  [the longest x5 60.2 us: norm_rows(): total = lax.psum(local_sq, 'ray')]
    pallas_call x0 -> x1, Pallas kernels: none -> 105 us  [local(): pl.pallas_call(functools.partial(kernel, R, C), out_shape=(jax.ShapeDtype...]
    dot_general x12 -> x0, matrix products: 29.3 us -> none  [the longest x4 16.1 us: local(): jnp.einsum('bsrc,nbsc->nbr', tiles, picked, preferred_element_type=jnp.fl...]
    reduce_sum x9 -> x0, other arithmetic: 9.93 us -> none  [the longest x5 5.13 us: local(): beta = norm_rows(jnp.sum(u_state * u_state, axis=1))]
    convert_element_type x9 -> x0, other arithmetic: 6.15 us -> none  [the longest x4 4.24 us: local(): vblocks = v_state.astype(jnp.bfloat16).reshape(nrhs, blocks, block_cells)]
  transfers between devices with their start and end apart: 8 -> 0, of which waited for: 8 -> 0; matrix products, arithmetic and copies ran while one was open for 0% -> 0% of each run, Pallas kernels for 0% -> 0%
where the time goes in v1:
time: 112 us
  Pallas kernels  105 us (94%)
  local copies, waits for them, and re-layouts  5.64 us (5%)
    pallas_call x1, Pallas kernels, local(): pl.pallas_call(functools.partial(kernel, R, C), out_shape=(jax.ShapeDtype...  105 us
    unnamed x3, local copies, waits for them, and re-layouts  4.33 us

profile of v1, /device:TPU:0, one launch (start us, length us, event | category | flops | bytes accessed | tf_op | source)
XLA Modules:
  0.0 111.6 jit_solution(18206484180795924659)
XLA Ops:
  0.6 1.3 %copy.8.pattern = s32[8,4]{1,0:T(8,128)} copy(s32[8,4]{0,1:T(4,128)} %param.6) | data formatting | bytes 256 | tf_op args[2]
  2.0 1.3 %copy.9.counts = s32[8,1]{1,0:T(8,128)} copy(s32[8,1]{0,1:T(1,128)} %param.7) | data formatting | bytes 64 | tf_op args[3]
  3.3 105.3 %shard_map.59 = (f32[8,8192]{1,0:T(8,128)}, f32[8,128]{1,0:T(8,128)}) custom-call(s32[8,4]{1,0:T(8,128)} %copy.8.pattern, s32[8,1]{1,0:T(8,128)} %copy.9.counts, f32[8,2048]{1,0:T(8,128)} %rhs.2, bf16[8,4,256,256]{3,2,1,0:T(8,128)(2,1)} %tiles_hbm.1), custom_call_target="tpu_custom_call" | custom-call | tf_op jit(solution)/shard_map/pallas_call | solution.py:296
  108.6 1.3 %slice_reduce_fusion = f32[8]{0:T(128)} fusion(f32[8,128]{1,0:T(8,128)} %get-tuple-element.5), kind=kLoop, calls=%fused_computation | loop fusion | bytes 64 | tf_op jit(solution)/shard_map/slice | solution.py:330
  109.9 1.7 %copy.11 = f32[8,8192]{1,0:T(8,128)} copy(f32[8,8192]{1,0:T(8,128)} %get-tuple-element.8) | data formatting | bytes 524288

commit v2 on v1

v2 whole, which is shorter than its diff:
```python
import functools

import jax
import jax.numpy as jnp
from jax import lax
from jax.experimental import pallas as pl
from jax.experimental.pallas import tpu as pltpu
from jax.sharding import PartitionSpec as P

BLK_DEV = 32
ITERS = 4
PIECES = 4
EPS = 1e-06
F32 = jnp.float32
BF16 = jnp.bfloat16


def split(value):
    hi = value.astype(BF16)
    lo = (value - hi.astype(F32)).astype(BF16)
    return hi, lo


def wide(stat, lanes):
    return jnp.broadcast_to(stat[:, 0:1], (stat.shape[0], lanes))


def eye(n):
    shape = (n, 128)
    return lax.broadcasted_iota(jnp.int32, shape, 0) == lax.broadcasted_iota(jnp.int32, shape, 1)


def to_row(value):
    n = value.shape[0]
    total = jnp.broadcast_to(jnp.sum(value, axis=1, keepdims=True), (n, 128))
    return jnp.sum(jnp.where(eye(n), total, 0.0), axis=0, keepdims=True)


def wide(row, n, lanes):
    spread = jnp.where(eye(n), jnp.broadcast_to(row, (n, 128)), 0.0)
    return jnp.broadcast_to(jnp.sum(spread, axis=1, keepdims=True), (n, lanes))


def kernel(
    R, C,
    pattern_hbm, counts_hbm, rhs, tiles_hbm,
    out, mis,
    tiles, flipped, fpart, frecv, ucat, apart, arecv, vhi, vlo, vsh, usq, vsq, gsq, cum, w, x,
    pattern, counts, idx, prv, lst,
    tile_sem, small_sem, fs, fr, us, ur, as_, ar, ns, nr, hs, hr, ls, lr, qs, qr, gs, gr,
):
    S, B = pattern.shape
    N = rhs.shape[0]
    RB, CB = tiles.shape[2], tiles.shape[3]
    RC = rhs.shape[1] // C
    NCH = C // B
    NB = BLK_DEV
    K = NB // R
    pieces = min(PIECES, K)
    KP = K // pieces
    slots = B * S
    me_r = lax.axis_index("ray")
    me_c = lax.axis_index("cell")

    small = [
        pltpu.make_async_copy(pattern_hbm, pattern, small_sem.at[0]),
        pltpu.make_async_copy(counts_hbm, counts, small_sem.at[1]),
    ]
    for copy in small:
        copy.start()
    loads = []
    for b in range(B):
        load = pltpu.make_async_copy(tiles_hbm.at[b], tiles.at[b], tile_sem.at[b])
        load.start()
        loads.append(load)

    barrier = pltpu.get_barrier_semaphore()
    for d in range(1, C):
        pl.semaphore_signal(barrier, inc=1, device_id={"cell": lax.rem(me_c + d, C)}, device_id_type=pl.DeviceIdType.MESH)
    for d in range(1, R):
        pl.semaphore_signal(barrier, inc=1, device_id={"ray": lax.rem(me_r + d, R)}, device_id_type=pl.DeviceIdType.MESH)

    def remote(src, dst, send, recv, axis, peer):
        return pltpu.make_async_remote_copy(
            src_ref=src, dst_ref=dst, send_sem=send, recv_sem=recv,
            device_id={axis: peer}, device_id_type=pl.DeviceIdType.MESH,
        )

    cum[slots] = jnp.zeros((N, CB), F32)
    vhi[0, NB] = jnp.zeros((N, CB), BF16)
    vhi[1, NB] = jnp.zeros((N, CB), BF16)
    w[...] = jnp.zeros_like(w)
    x[...] = jnp.zeros_like(x)
    vsh[...] = jnp.zeros_like(vsh)
    for j in range(C):
        hi, lo = split(rhs[:, j * RC:(j + 1) * RC])
        ucat[j, 0:N] = hi
        ucat[j, N:2 * N] = lo

    for copy in small:
        copy.wait()
    for b in range(B):
        for s in range(S):
            idx[b * S + s] = jnp.where(s < counts[0, b], pattern[s, b], NB)

    def chain(i, carry):
        p = idx[i]
        found = jnp.int32(slots)
        for j in range(slots):
            found = jnp.where((idx[j] == p) & (j < i), j, found)
        prv[i] = found
        return carry

    lax.fori_loop(0, slots, chain, 0)

    def final(k, carry):
        found = jnp.int32(slots)
        for j in range(slots):
            found = jnp.where(idx[j] == k, j, found)
        lst[k] = found
        return carry

    lax.fori_loop(0, NB, final, 0)

    order = sorted(range(1, R), key=lambda d: abs(d - R // 2))

    def ray_peer(d):
        return lax.rem(me_r + d, R)

    def slot_copies(ref, send, recv):
        return [remote(ref.at[me_r], ref.at[me_r], send.at[d], recv.at[d], "ray", ray_peer(d)) for d in order]

    def cell_copies(ref, send, recv):
        return [
            remote(ref.at[me_c], ref.at[me_c], send.at[d], recv.at[d], "cell", lax.rem(me_c + d, C))
            for d in range(1, C)
        ]

    def rows_copies(ref, send, recv, start, count, p):
        own = ref.at[pl.ds(me_r * K + start, count)]
        return [remote(own, own, send.at[d, p], recv.at[d, p], "ray", ray_peer(d)) for d in order]

    def scatter_copies(p):
        return [
            remote(
                apart.at[pl.ds(ray_peer(d) * K + p * KP, KP)], arecv.at[me_r, pl.ds(p * KP, KP)],
                as_.at[d, p], ar.at[d, p], "ray", ray_peer(d),
            )
            for d in order
        ]

    def norm_start():
        sq = jnp.zeros((N, RC), F32)
        for j in range(C):
            u = ucat[j, 0:N].astype(F32) + ucat[j, N:2 * N].astype(F32)
            sq = sq + u * u
        usq[me_r] = to_row(sq)
        copies = slot_copies(usq, ns, nr)
        for copy in copies:
            copy.start()
        return copies

    def norm_end(copies):
        for copy in copies:
            copy.wait()
        total = usq[0]
        for r in range(1, R):
            total = total + usq[r]
        return jnp.sqrt(total + EPS)

    def adjoint(wait):
        for b in range(B):
            if wait:
                loads[b].wait()
            if NCH == 1:
                rows = ucat[b]
            else:
                rows = jnp.concatenate([ucat[b * NCH + h] for h in range(NCH)], axis=1)
            for s in range(S):
                i = b * S + s
                per = lax.dot_general(rows, tiles[b, s], (((1,), (0,)), ((), ())), preferred_element_type=F32)
                cum[i] = per[0:N] + per[N:2 * N] + cum[prv[i]]
        for k in range(NB):
            apart[k] = cum[lst[k]]

    def scatter_start():
        for p in range(pieces):
            for copy in scatter_copies(p):
                copy.start()
        arecv[me_r] = apart[pl.ds(me_r * K, K)]

    def gather(beta, alpha, side, beside):
        inv = wide(1.0 / beta, N, CB)
        back = wide(beta / alpha, N, CB)
        sq = jnp.zeros((N, CB), F32)
        for p in range(pieces):
            for copy in scatter_copies(p):
                copy.wait_recv()
            for k in range(p * KP, (p + 1) * KP):
                total = arecv[0, k]
                for r in range(1, R):
                    total = total + arecv[r, k]
                v = total * inv - back * vsh[k]
                vsh[k] = v
                sq = sq + v * v
                hi, lo = split(v)
                vhi[side, me_r * K + k] = hi
                vlo[side, me_r * K + k] = lo
            if p == pieces - 1:
                vsq[me_r] = to_row(sq)
                for copy in slot_copies(vsq, qs, qr):
                    copy.start()
            for copy in rows_copies(vhi.at[side], hs, hr, p * KP, KP, p):
                copy.start()
        beside()
        for p in range(pieces):
            for copy in scatter_copies(p):
                copy.wait_send()
        for copy in slot_copies(vsq, qs, qr):
            copy.wait()
        group = vsq[0]
        for r in range(1, R):
            group = group + vsq[r]
        gsq[me_c] = group
        for copy in cell_copies(gsq, gs, gr):
            copy.start()
        for p in range(pieces):
            for copy in rows_copies(vhi.at[side], hs, hr, p * KP, KP, p):
                copy.wait()
        for copy in rows_copies(vlo.at[side], ls, lr, 0, K, 0):
            copy.start()

    def forward(beta, side):
        mine = me_c // NCH
        for t in range(B):
            b = lax.rem(mine + 1 + t, B)
            acc = jnp.zeros((N, RB), F32)
            for s in range(S):
                acc = acc + lax.dot_general(
                    vhi[side, idx[b * S + s]], flipped[b, s], (((1,), (0,)), ((), ())), preferred_element_type=F32
                )
            for h in range(NCH):
                j = b * NCH + h
                fpart[j] = acc[:, h * RC:(h + 1) * RC]
                d = lax.rem(j - me_c + C, C)

                @pl.when(j != me_c)
                def _():
                    remote(fpart.at[j], frecv.at[me_c], fs.at[d], fr.at[d], "cell", j).start()

        frecv[me_c] = fpart[me_c]
        for copy in cell_copies(gsq, gs, gr):
            copy.wait()
        norm = gsq[0]
        for j in range(1, C):
            norm = norm + gsq[j]
        alpha = jnp.sqrt(norm + EPS)
        inv = wide(1.0 / alpha, N, RC)
        old = ucat[me_c, 0:N].astype(F32) + ucat[me_c, N:2 * N].astype(F32)
        old = wide(alpha / beta, N, RC) * old
        for d in range(1, C):
            peer = lax.rem(me_c + d, C)
            remote(fpart.at[peer], frecv.at[me_c], fs.at[d], fr.at[d], "cell", peer).wait()
        total = frecv[0]
        for j in range(1, C):
            total = total + frecv[j]
        hi, lo = split(total * inv - old)
        ucat[me_c, 0:N] = hi
        ucat[me_c, N:2 * N] = lo
        copies = cell_copies(ucat, us, ur)
        for copy in copies:
            copy.start()
        for copy in copies:
            copy.wait()
        return alpha

    def step_w(alpha, sine, rho, side):
        for copy in rows_copies(vlo.at[side], ls, lr, 0, K, 0):
            copy.wait()
        inv = wide(1.0 / alpha, N, CB)
        ratio = wide(sine * alpha / rho, N, CB)
        for k in range(NB):
            w[k] = (vhi[side, k].astype(F32) + vlo[side, k].astype(F32)) * inv - ratio * w[k]

    def rotate(beta, rhobar, phibar):
        rho = jnp.sqrt(rhobar * rhobar + beta * beta)
        cosine = rhobar / rho
        sine = beta / rho
        phi = cosine * phibar
        return rho, cosine, sine, sine * phibar, phi / rho

    def flip():
        def one(i, carry):
            for s in range(S):
                flipped[i, s] = tiles[i, s].T
            return carry

        lax.fori_loop(0, B, one, 0)

    adjoint(True)
    pl.semaphore_wait(barrier, (C - 1) + (R - 1))
    norms = norm_start()
    scatter_start()
    flip()
    beta = norm_end(norms)
    one = jnp.ones((1, 128), F32)
    gather(beta, one, 0, lambda: None)

    def body(step, carry):
        beta, cosine, sine, rho, phibar = carry
        side = lax.rem(step, 2)
        alpha = forward(beta, side)
        norms = norm_start()
        adjoint(False)
        scatter_start()
        step_w(alpha, sine, rho, side)
        beta = norm_end(norms)
        rho, cosine, sine, phibar, length = rotate(beta, -cosine * alpha, phibar)

        def step_x():
            scale = wide(length, N, CB)
            for k in range(NB):
                x[k] = x[k] + scale * w[k]

        gather(beta, alpha, 1 - side, step_x)
        return beta, cosine, sine, rho, phibar

    carry = (beta, -one, jnp.zeros((1, 128), F32), one, beta)
    beta, cosine, sine, rho, phibar = lax.fori_loop(0, ITERS - 1, body, carry)
    side = (ITERS - 1) % 2
    alpha = forward(beta, side)
    norms = norm_start()
    step_w(alpha, sine, rho, side)
    beta = norm_end(norms)
    rho, cosine, sine, phibar, length = rotate(beta, -cosine * alpha, phibar)
    scale = wide(length, N, CB)
    for k in range(NB):
        out[:, k * CB:(k + 1) * CB] = x[k] + scale * w[k]
    mis[...] = phibar


def local(R, C, right_side, tiles, pattern, counts):
    N, rows = right_side.shape
    B, S, RB, CB = tiles.shape
    NB = BLK_DEV
    RC = rows // C
    K = NB // R
    pieces = min(PIECES, K)
    slots = B * S
    vmem = pl.BlockSpec(memory_space=pltpu.VMEM)
    hbm = pl.BlockSpec(memory_space=pl.ANY)
    dma = pltpu.SemaphoreType.DMA
    x, mis = pl.pallas_call(
        functools.partial(kernel, R, C),
        out_shape=(
            jax.ShapeDtypeStruct((N, NB * CB), F32),
            jax.ShapeDtypeStruct((1, 128), F32),
        ),
        in_specs=[hbm, hbm, vmem, hbm],
        out_specs=(vmem, vmem),
        scratch_shapes=[
            pltpu.VMEM((B, S, RB, CB), BF16),
            pltpu.VMEM((B, S, CB, RB), BF16),
            pltpu.VMEM((C, N, RC), F32),
            pltpu.VMEM((C, N, RC), F32),
            pltpu.VMEM((C, 2 * N, RC), BF16),
            pltpu.VMEM((NB, N, CB), F32),
            pltpu.VMEM((R, K, N, CB), F32),
            pltpu.VMEM((2, NB + 1, N, CB), BF16),
            pltpu.VMEM((2, NB, N, CB), BF16),
            pltpu.VMEM((K, N, CB), F32),
            pltpu.VMEM((R, 1, 128), F32),
            pltpu.VMEM((R, 1, 128), F32),
            pltpu.VMEM((C, 1, 128), F32),
            pltpu.VMEM((slots + 1, N, CB), F32),
            pltpu.VMEM((NB, N, CB), F32),
            pltpu.VMEM((NB, N, CB), F32),
            pltpu.SMEM((S, B), jnp.int32),
            pltpu.SMEM((1, B), jnp.int32),
            pltpu.SMEM((slots,), jnp.int32),
            pltpu.SMEM((slots,), jnp.int32),
            pltpu.SMEM((NB,), jnp.int32),
            dma((B,)), dma((2,)),
            dma((C,)), dma((C,)), dma((C,)), dma((C,)),
            dma((R, pieces)), dma((R, pieces)), dma((R,)), dma((R,)),
            dma((R, pieces)), dma((R, pieces)), dma((R, 1)), dma((R, 1)),
            dma((R,)), dma((R,)), dma((C,)), dma((C,)),
        ],
        compiler_params=pltpu.CompilerParams(collective_id=0, has_side_effects=True),
    )(pattern.T, counts.T, right_side, tiles)
    return x, mis[0, :N]


def solution(mesh):
    R, C = mesh.shape["ray"], mesh.shape["cell"]
    in_specs = (P(None, "ray"), P("ray", "cell", None, None), P("ray", "cell"), P("ray", "cell"))
    out_specs = (P(None, "cell"), P())
    return jax.shard_map(
        functools.partial(local, R, C), mesh=mesh, in_specs=in_specs, out_specs=out_specs, check_vma=False
    )
```

time: 112 us -> 102 us (0.911)
  Pallas kernels: 105 us -> 98 us
  local copies, waits for them, and re-layouts: 5.64 us -> 2.8 us
    pallas_call x1, Pallas kernels: 105 us -> 98 us  [local(): pl.pallas_call(functools.partial(kernel, R, C), out_shape=(jax.ShapeDtype...]
    unnamed x3 -> x1, local copies, waits for them, and re-layouts: 4.33 us -> 1.67 us
    slice x1 -> x0, local copies, waits for them, and re-layouts: 1.31 us -> none  [local(): return (x, mis[:, 0])]
    squeeze x0 -> x1, local copies, waits for them, and re-layouts: none -> 1.13 us  [local(): return (x, mis[0, :N])]
where the time goes in v2:
time: 102 us; the launch traced here: 101 us
  Pallas kernels  98 us (96%)
  local copies, waits for them, and re-layouts  2.8 us (3%)
    pallas_call x1, Pallas kernels, local(): pl.pallas_call(functools.partial(kernel, R, C), out_shape=(jax.ShapeDtype...  98 us

profile of v2, /device:TPU:0, one launch (start us, length us, event | category | flops | bytes accessed | tf_op | source)
XLA Modules:
  0.0 101.5 jit_solution(3582533457843600819)
XLA Ops:
  0.6 98.0 %shard_map.59 = (f32[8,8192]{1,0:T(8,128)}, f32[1,128]{1,0:T(1,128)}) custom-call(s32[4,8]{1,0:T(4,128)} %bitcast.4, s32[1,8]{1,0:T(1,128)} %bitcast.5, f32[8,2048]{1,0:T(8,128)} %rhs.1, bf16[8,4,256,256]{3,2,1,0:T(8,128)(2,1)} %tiles_hbm.1), custom_call_target="tpu_custom_call" | custom-call | tf_op jit(solution)/shard_map/pallas_call | solution.py:353
  98.7 1.1 %slice_bitcast_fusion = f32[8]{0:T(128)} fusion(f32[1,128]{1,0:T(1,128)} %get-tuple-element.5), kind=kLoop, calls=%fused_computation | loop fusion | bytes 64 | tf_op jit(solution)/shard_map/squeeze | solution.py:391
  99.8 1.7 %copy.7 = f32[8,8192]{1,0:T(8,128)} copy(f32[8,8192]{1,0:T(8,128)} %get-tuple-element.8) | data formatting | bytes 524288

commit v3 on v2

--- a/solution.py
+++ b/solution.py
@@ -9,7 +9,7 @@
 
 BLK_DEV = 32
 ITERS = 4
-PIECES = 4
+PIECES = 1
 EPS = 1e-06
 F32 = jnp.float32
 BF16 = jnp.bfloat16
@@ -231,22 +231,17 @@
             copy.start()
 
     def forward(beta, side):
-        mine = me_c // NCH
-        for t in range(B):
-            b = lax.rem(mine + 1 + t, B)
+        for b in range(B):
             acc = jnp.zeros((N, RB), F32)
             for s in range(S):
                 acc = acc + lax.dot_general(
                     vhi[side, idx[b * S + s]], flipped[b, s], (((1,), (0,)), ((), ())), preferred_element_type=F32
                 )
             for h in range(NCH):
-                j = b * NCH + h
-                fpart[j] = acc[:, h * RC:(h + 1) * RC]
-                d = lax.rem(j - me_c + C, C)
-
-                @pl.when(j != me_c)
-                def _():
-                    remote(fpart.at[j], frecv.at[me_c], fs.at[d], fr.at[d], "cell", j).start()
+                fpart[b * NCH + h] = acc[:, h * RC:(h + 1) * RC]
+        for d in range(1, C):
+            peer = lax.rem(me_c + d, C)
+            remote(fpart.at[peer], frecv.at[me_c], fs.at[d], fr.at[d], "cell", peer).start()
 
         frecv[me_c] = fpart[me_c]
         for copy in cell_copies(gsq, gs, gr):

time: 102 us -> 94.8 us (0.929)
  Pallas kernels: 98 us -> 91.2 us
    pallas_call x1, Pallas kernels: 98 us -> 91.2 us  [local(): pl.pallas_call(functools.partial(kernel, R, C), out_shape=(jax.ShapeDtype...]
where the time goes in v3:
time: 94.8 us; the launch traced here: 94.6 us
  Pallas kernels  91.2 us (96%)
  local copies, waits for them, and re-layouts  2.8 us (3%)
    pallas_call x1, Pallas kernels, local(): pl.pallas_call(functools.partial(kernel, R, C), out_shape=(jax.ShapeDtype...  91.2 us

profile of v3, /device:TPU:0, one launch (start us, length us, event | category | flops | bytes accessed | tf_op | source)
XLA Modules:
  0.0 94.6 jit_solution(4979277579828560132)
XLA Ops:
  0.6 91.2 %shard_map.59 = (f32[8,8192]{1,0:T(8,128)}, f32[1,128]{1,0:T(1,128)}) custom-call(s32[4,8]{1,0:T(4,128)} %bitcast.4, s32[1,8]{1,0:T(1,128)} %bitcast.5, f32[8,2048]{1,0:T(8,128)} %rhs.1, bf16[8,4,256,256]{3,2,1,0:T(8,128)(2,1)} %tiles_hbm.1), custom_call_target="tpu_custom_call" | custom-call | tf_op jit(solution)/shard_map/pallas_call | solution.py:348
  91.8 1.1 %slice_bitcast_fusion = f32[8]{0:T(128)} fusion(f32[1,128]{1,0:T(1,128)} %get-tuple-element.5), kind=kLoop, calls=%fused_computation | loop fusion | bytes 64 | tf_op jit(solution)/shard_map/squeeze | solution.py:386
  93.0 1.7 %copy.7 = f32[8,8192]{1,0:T(8,128)} copy(f32[8,8192]{1,0:T(8,128)} %get-tuple-element.8) | data formatting | bytes 524288
